TPU v7x, 32 devices: a whole 2x2x4 slice. The times are simulated.
32 devices in a mesh: rep: 4 (over y, x), seq: 8 (over z, core).
Axes of the slice: x: 2, y: 2, z: 4, core: 2. Of those that a mesh axis runs over, the one named last changes fastest.
Arguments:
- inputs: bfloat16 [4, 2048, 1536], P('rep', 'seq'), may hold values from -13 to 13
- segment_ids: int32 [4, 2048], P('rep'), may hold values from 0 to 7, as said below
- valid_mask: int32 [4, 2048], P('rep'), may hold values from 0 to 1, as said below
- input_weight: bfloat16 [1536, 4608], P('seq'), may hold values from -0.15625 to 0.15625
- output_weight: bfloat16 [1536, 1536], P('seq'), may hold values from -0.15625 to 0.15625
- conv_kernel: float32 [16, 6, 11], replicated, may hold values from -1.2 to 1.2
- head_mix: float32 [8, 2, 2], replicated, may hold values from 0.2 to 1
- first_gain: float32 [1536], replicated, may hold values from 0.5 to 1.5
- second_gain: float32 [1536], replicated, may hold values from 0.5 to 1.5
- group_gain: float32 [1536], replicated, may hold values from 0.5 to 1.5
- gate_weight: bfloat16 [1536, 4096], P(None, 'seq'), may hold values from -0.15625 to 0.15625
- up_weight: bfloat16 [1536, 4096], P(None, 'seq'), may hold values from -0.15625 to 0.15625
- down_weight: bfloat16 [4096, 1536], P('seq'), may hold values from -0.09375 to 0.09375
- cotangent: bfloat16 [4, 2048, 1536], P('rep', 'seq'), may hold values from -17 to 17
Outputs:
- output: bfloat16 [4, 2048, 1536], P('rep', 'seq')
- grad_inputs: bfloat16 [4, 2048, 1536], P('rep', 'seq')
- grad_input_weight: float32 [1536, 4608], P('seq')
- grad_output_weight: float32 [1536, 1536], P('seq')
- grad_kernel: float32 [16, 6, 11], replicated
- grad_mix: float32 [8, 2, 2], replicated
- grad_first_gain: float32 [1536], replicated
- grad_second_gain: float32 [1536], replicated
- grad_group_gain: float32 [1536], replicated
- grad_gate: float32 [1536, 4096], P(None, 'seq')
- grad_up: float32 [1536, 4096], P(None, 'seq')
- grad_down: float32 [4096, 1536], P('seq')
Inputs may be any that keep to these rules, and one draw needn't show every extreme that they name: `segment_ids`: segment ids never fall along a sequence and start at 0. The positions k * 1024 to (k + 1) * 1024 - 1 form frame k; every document lies inside one frame, a frame holds one to four documents, the first frame of the first sequence is a single document of exactly 1024 positions, and every frame of the last sequence holds four documents. `valid_mask`: in each frame the positions with 0 form its tail, at most 256 of them; the first frame of the first sequence has none.
All inputs are finite; a program needn't handle non-finite values.
Results may differ from a plain program's by a relative error of at most 0.02.
Values may be sent and summed in bfloat16 or wider, within the bound.
A program may use at most 384 MiB of HBM per device.

v0:
```python
import jax
import jax.numpy as jnp
from jax import lax
from jax.sharding import PartitionSpec as P

REACH = 4
EPS = 1e-06
HIGHEST = lax.Precision.HIGHEST


def from_behind(x, axis, by):
    count = lax.axis_size(axis)
    pairs = [(i, i + by) for i in range(count) if 0 <= i + by < count]
    return lax.ppermute(x, axis, pairs)


def convolve(logits, kernel, rows, columns):
    rim_rows = kernel.shape[1] - 1
    key_span = kernel.shape[2] - 1
    result = jnp.zeros((logits.shape[0], rows, columns), jnp.float32)
    for row_tap in range(kernel.shape[1]):
        for col_tap in range(kernel.shape[2]):
            weight = kernel[:, row_tap, col_tap][:, None, None]
            result = (
                result
                + weight
                * logits[
                    :,
                    rim_rows - row_tap : rim_rows - row_tap + rows,
                    key_span - col_tap : key_span - col_tap + columns,
                ]
            )
    return result


def convolve_back(grads, kernel):
    rim_rows = kernel.shape[1] - 1
    key_span = kernel.shape[2] - 1
    rows = grads.shape[1] + rim_rows
    columns = grads.shape[2] + key_span
    padded = jnp.pad(grads, ((0, 0), (rim_rows, rim_rows), (key_span, key_span)))
    result = jnp.zeros((grads.shape[0], rows, columns), jnp.float32)
    for row_tap in range(kernel.shape[1]):
        for col_tap in range(kernel.shape[2]):
            weight = kernel[:, row_tap, col_tap][:, None, None]
            result = (
                result + weight * padded[:, row_tap : row_tap + rows, col_tap : col_tap + columns]
            )
    return result


def kernel_grads(grads, logits, taps_rows, taps_cols):
    rim_rows = taps_rows - 1
    key_span = taps_cols - 1
    rows = grads.shape[1]
    columns = grads.shape[2]
    entries = []
    for row_tap in range(taps_rows):
        line_sums = []
        for col_tap in range(taps_cols):
            window_part = logits[
                :,
                rim_rows - row_tap : rim_rows - row_tap + rows,
                key_span - col_tap : key_span - col_tap + columns,
            ]
            line_sums.append(jnp.sum(grads * window_part, axis=(1, 2)))
        entries.append(jnp.stack(line_sums, axis=-1))
    return jnp.stack(entries, axis=1)


def attend_group(operands, mask_ext, mask_own, row_valid, score_scale):
    query_g, key_g, value_g, kernel_g, mixing_g = operands
    rows = mask_own.shape[0]
    columns = mask_own.shape[1]
    raw = jnp.einsum("qhd,khd->hqk", query_g, key_g, preferred_element_type=jnp.float32)
    logits = raw * score_scale * mask_ext
    conv = convolve(logits, kernel_g, rows, columns)
    allowed = mask_own > 0
    peak = jnp.max(jnp.where(allowed, conv, -1e30), axis=-1, keepdims=True)
    peak = jnp.where(row_valid > 0, peak, 0.0)
    expo = jnp.where(allowed, jnp.exp(conv - peak), 0.0)
    denom = jnp.sum(expo, axis=-1, keepdims=True) + 1.0 - row_valid
    prob = expo / denom
    mixed = (
        mixing_g[:, 0][:, None, None] * prob[0][None]
        + mixing_g[:, 1][:, None, None] * prob[1][None]
    )
    mixed_low = mixed.astype(jnp.bfloat16)
    result = jnp.einsum("hqk,khd->qhd", mixed_low, value_g, preferred_element_type=jnp.float32)
    return (result, peak + jnp.log(denom))


def attend_group_back(operands, mask_ext, mask_own, score_scale):
    query_g, key_g, value_g, kernel_g, mixing_g, dresult_g, lse_g = operands
    rows = mask_own.shape[0]
    columns = mask_own.shape[1]
    raw = jnp.einsum("qhd,khd->hqk", query_g, key_g, preferred_element_type=jnp.float32)
    logits = raw * score_scale * mask_ext
    conv = convolve(logits, kernel_g, rows, columns)
    allowed = mask_own > 0
    prob = jnp.where(allowed, jnp.exp(conv - lse_g), 0.0)
    mixed = (
        mixing_g[:, 0][:, None, None] * prob[0][None]
        + mixing_g[:, 1][:, None, None] * prob[1][None]
    )
    mixed_low = mixed.astype(jnp.bfloat16)
    dmixed = jnp.einsum("qhd,khd->hqk", dresult_g, value_g, preferred_element_type=jnp.float32)
    dvalue = jnp.einsum("hqk,qhd->khd", mixed_low, dresult_g, preferred_element_type=jnp.float32)
    dmixing = jnp.stack(
        [
            jnp.sum(dmixed * prob[0][None], axis=(1, 2)),
            jnp.sum(dmixed * prob[1][None], axis=(1, 2)),
        ],
        axis=-1,
    )
    dprob = (
        mixing_g[0][:, None, None] * dmixed[0][None] + mixing_g[1][:, None, None] * dmixed[1][None]
    )
    dconv = prob * (dprob - jnp.sum(prob * dprob, axis=-1, keepdims=True))
    dkernel = kernel_grads(dconv, logits, kernel_g.shape[1], kernel_g.shape[2])
    dlogits = convolve_back(dconv, kernel_g) * mask_ext * score_scale
    dquery = jnp.einsum(
        "hqk,khd->qhd",
        dlogits,
        key_g.astype(jnp.float32),
        precision=HIGHEST,
        preferred_element_type=jnp.float32,
    )
    dkey = jnp.einsum(
        "hqk,qhd->khd",
        dlogits,
        query_g.astype(jnp.float32),
        precision=HIGHEST,
        preferred_element_type=jnp.float32,
    )
    return (dquery, dkey, dvalue, dkernel, dmixing)


def rms_scale(values):
    return lax.rsqrt(jnp.mean(values * values, axis=-1, keepdims=True) + EPS)


def norm_back(grad_out, values, inv_scale, gain):
    scaled_grad = grad_out * gain
    inner = jnp.mean(scaled_grad * values, axis=-1, keepdims=True)
    return inv_scale * scaled_grad - values * inv_scale**3 * inner


def on_device(
    inputs,
    segment_ids,
    valid_mask,
    input_weight,
    output_weight,
    conv_kernel,
    head_mix,
    first_gain,
    second_gain,
    group_gain,
    gate_weight,
    up_weight,
    down_weight,
    cotangent,
):
    tokens = inputs.shape[1]
    model_width = inputs.shape[2]
    head_count = conv_kernel.shape[0]
    head_dim = model_width // head_count
    groups = head_mix.shape[0]
    rim_rows = conv_kernel.shape[1] - 1
    half_span = conv_kernel.shape[2] // 2
    window = REACH * tokens
    score_scale = head_dim ** (-0.5)
    seq_rank = lax.axis_index("seq")
    row_start = seq_rank * tokens
    window_start = row_start - (REACH - 1) * tokens
    resid_in = inputs[0].astype(jnp.float32)
    grad_out = cotangent[0].astype(jnp.float32)
    offset = window + half_span
    segment_pad = jnp.concatenate(
        [jnp.full((offset,), -1, jnp.int32), segment_ids[0], jnp.full((half_span,), -1, jnp.int32)]
    )
    valid_pad = jnp.concatenate(
        [jnp.zeros((offset,), jnp.int32), valid_mask[0], jnp.zeros((half_span,), jnp.int32)]
    )
    query_pos = row_start - rim_rows + jnp.arange(tokens + rim_rows, dtype=jnp.int32)
    key_pos = window_start - half_span + jnp.arange(window + 2 * half_span, dtype=jnp.int32)
    query_seg = lax.dynamic_slice_in_dim(
        segment_pad, row_start - rim_rows + offset, tokens + rim_rows
    )
    key_seg = lax.dynamic_slice_in_dim(
        segment_pad, window_start - half_span + offset, window + 2 * half_span
    )
    query_live = lax.dynamic_slice_in_dim(
        valid_pad, row_start - rim_rows + offset, tokens + rim_rows
    )
    key_live = lax.dynamic_slice_in_dim(
        valid_pad, window_start - half_span + offset, window + 2 * half_span
    )
    mask_ext = (
        (query_seg[:, None] == key_seg[None, :])
        & (key_pos[None, :] <= query_pos[:, None])
        & (query_live[:, None] > 0)
        & (key_live[None, :] > 0)
    ).astype(jnp.float32)
    mask_own = mask_ext[rim_rows:, half_span : half_span + window]
    row_valid = query_live[rim_rows:].astype(jnp.float32)[:, None]
    full_input, full_output = (
        lax.all_gather(input_weight, "seq", axis=0, tiled=True),
        lax.all_gather(output_weight, "seq", axis=0, tiled=True),
    )
    first_scale = rms_scale(resid_in)
    normed_in = (resid_in * first_scale * first_gain).astype(jnp.bfloat16)
    projected = jnp.dot(normed_in, full_input, preferred_element_type=jnp.float32).astype(
        jnp.bfloat16
    )
    query = projected[:, :model_width]
    keys_values = projected[:, model_width:]
    query_rim = from_behind(query[tokens - rim_rows :], "seq", 1)
    query_ext = jnp.concatenate([query_rim, query], axis=0)
    pieces = [keys_values]
    for distance in range(1, REACH):
        pieces.append(from_behind(keys_values, "seq", distance))
    window_rows = jnp.concatenate(pieces[::-1], axis=0)
    key_ext = jnp.pad(window_rows[:, :model_width], ((half_span, half_span), (0, 0)))
    value_window = window_rows[:, model_width:]

    def split_heads(values):
        return values.reshape(values.shape[0], groups, 2, head_dim).transpose(1, 0, 2, 3)

    def merge_heads(values):
        return values.transpose(1, 0, 2, 3).reshape(values.shape[1], model_width)

    query_groups = split_heads(query_ext)
    key_groups = split_heads(key_ext)
    value_groups = split_heads(value_window)
    kernel_groups = conv_kernel.reshape(groups, 2, conv_kernel.shape[1], conv_kernel.shape[2])
    result_groups, lse_groups = lax.map(
        lambda operands: attend_group(operands, mask_ext, mask_own, row_valid, score_scale),
        (query_groups, key_groups, value_groups, kernel_groups, head_mix),
    )
    attended = merge_heads(result_groups)
    shaped = attended.reshape(tokens, head_count, head_dim)
    centred = shaped - jnp.mean(shaped, axis=-1, keepdims=True)
    inv_std = lax.rsqrt(jnp.mean(centred * centred, axis=-1, keepdims=True) + EPS)
    unit_heads = centred * inv_std
    unit = unit_heads.reshape(tokens, model_width)
    normed = (unit * group_gain).astype(jnp.bfloat16)
    branch = jnp.dot(normed, full_output, preferred_element_type=jnp.float32)
    resid = resid_in + row_valid * branch
    second_scale = rms_scale(resid)
    normed_mid = (resid * second_scale * second_gain).astype(jnp.bfloat16)
    dmlp = (row_valid * grad_out).astype(jnp.bfloat16)
    contract_rows = (((0,), (0,)), ((), ()))
    inputs_all = lax.all_gather(normed_mid, "seq", axis=0, tiled=True)
    gate = jnp.dot(inputs_all, gate_weight, preferred_element_type=jnp.float32)
    up_proj = jnp.dot(inputs_all, up_weight, preferred_element_type=jnp.float32)
    hidden = (jax.nn.silu(gate) * up_proj).astype(jnp.bfloat16)
    mlp = lax.psum_scatter(
        jnp.dot(hidden, down_weight, preferred_element_type=jnp.float32).astype(jnp.bfloat16),
        "seq",
        scatter_dimension=0,
        tiled=True,
    ).astype(jnp.float32)
    result = resid + row_valid * mlp
    dmlp_all = lax.all_gather(dmlp, "seq", axis=0, tiled=True)
    dhidden = jnp.dot(dmlp_all, down_weight.T, preferred_element_type=jnp.float32)
    sigmoid_gate = jax.nn.sigmoid(gate)
    gate_grad = (dhidden * up_proj * sigmoid_gate * (1.0 + gate * (1.0 - sigmoid_gate))).astype(
        jnp.bfloat16
    )
    up_grad = (dhidden * gate * sigmoid_gate).astype(jnp.bfloat16)
    grad_down = lax.dot_general(hidden, dmlp_all, contract_rows, preferred_element_type=jnp.float32)
    grad_gate = lax.dot_general(
        inputs_all, gate_grad, contract_rows, preferred_element_type=jnp.float32
    )
    grad_up = lax.dot_general(
        inputs_all, up_grad, contract_rows, preferred_element_type=jnp.float32
    )
    dmid = lax.psum_scatter(
        (
            jnp.dot(gate_grad, gate_weight.T, preferred_element_type=jnp.float32)
            + jnp.dot(up_grad, up_weight.T, preferred_element_type=jnp.float32)
        ).astype(jnp.bfloat16),
        "seq",
        scatter_dimension=0,
        tiled=True,
    ).astype(jnp.float32)
    second_part = jnp.sum(dmid * resid * second_scale, axis=0)
    dresid = grad_out + norm_back(dmid, resid, second_scale, second_gain)
    dbranch = (row_valid * dresid).astype(jnp.bfloat16)
    whole_output_grad = lax.dot_general(
        normed, dbranch, contract_rows, preferred_element_type=jnp.float32
    )
    dnormed = jnp.dot(dbranch, full_output.T, preferred_element_type=jnp.float32)
    group_part = jnp.sum(dnormed * unit, axis=0)
    dunit = (dnormed * group_gain).reshape(tokens, head_count, head_dim)
    dshaped = inv_std * (
        dunit
        - jnp.mean(dunit, axis=-1, keepdims=True)
        - unit_heads * jnp.mean(dunit * unit_heads, axis=-1, keepdims=True)
    )
    dattended = dshaped.reshape(tokens, model_width).astype(jnp.bfloat16)
    dquery_g, dkey_g, dvalue_g, dkernel_g, dmixing = lax.map(
        lambda operands: attend_group_back(operands, mask_ext, mask_own, score_scale),
        (
            query_groups,
            key_groups,
            value_groups,
            kernel_groups,
            head_mix,
            split_heads(dattended),
            lse_groups,
        ),
    )
    dquery_ext = merge_heads(dquery_g)
    dkey_window = merge_heads(dkey_g)[half_span : half_span + window]
    dvalue_window = merge_heads(dvalue_g)
    dpair_window = jnp.concatenate([dkey_window, dvalue_window], axis=1)
    dpair = dpair_window[(REACH - 1) * tokens :]
    for distance in range(1, REACH):
        block_first = (REACH - 1 - distance) * tokens
        dpair = dpair + from_behind(
            dpair_window[block_first : block_first + tokens].astype(jnp.bfloat16), "seq", -distance
        ).astype(jnp.float32)
    rim_grad = from_behind(dquery_ext[:rim_rows], "seq", -1)
    dquery_own = dquery_ext[rim_rows:]
    dquery_own = jnp.concatenate(
        [dquery_own[: tokens - rim_rows], dquery_own[tokens - rim_rows :] + rim_grad], axis=0
    )
    dprojected = jnp.concatenate([dquery_own, dpair], axis=1).astype(jnp.bfloat16)
    whole_input_grad = lax.dot_general(
        normed_in, dprojected, contract_rows, preferred_element_type=jnp.float32
    )
    dnormin = jnp.dot(dprojected, full_input.T, preferred_element_type=jnp.float32)
    first_part = jnp.sum(dnormin * resid_in * first_scale, axis=0)
    grad_in = dresid + norm_back(dnormin, resid_in, first_scale, first_gain)
    input_shard, output_shard = (
        lax.psum_scatter(
            whole_input_grad.astype(jnp.bfloat16), "seq", scatter_dimension=0, tiled=True
        ).astype(jnp.float32),
        lax.psum_scatter(
            whole_output_grad.astype(jnp.bfloat16), "seq", scatter_dimension=0, tiled=True
        ).astype(jnp.float32),
    )
    kernel_part = dkernel_g.reshape(head_count, conv_kernel.shape[1], conv_kernel.shape[2])
    grad_kernel, grad_mix, grad_first, grad_second, grad_group = lax.psum(
        (kernel_part, dmixing, first_part, second_part, group_part), ("rep", "seq")
    )
    grad_input_w, grad_output_w, grad_gate, grad_up, grad_down = (
        lax.psum(input_shard.astype(jnp.bfloat16), "rep").astype(jnp.float32),
        lax.psum(output_shard.astype(jnp.bfloat16), "rep").astype(jnp.float32),
        lax.psum(grad_gate.astype(jnp.bfloat16), "rep").astype(jnp.float32),
        lax.psum(grad_up.astype(jnp.bfloat16), "rep").astype(jnp.float32),
        lax.psum(grad_down.astype(jnp.bfloat16), "rep").astype(jnp.float32),
    )
    return (
        result.astype(jnp.bfloat16)[None],
        grad_in.astype(jnp.bfloat16)[None],
        grad_input_w,
        grad_output_w,
        grad_kernel,
        grad_mix,
        grad_first,
        grad_second,
        grad_group,
        grad_gate,
        grad_up,
        grad_down,
    )


def solution(mesh):
    in_specs = (
        P("rep", "seq", None),
        P("rep", None),
        P("rep", None),
        P("seq", None),
        P("seq", None),
        P(),
        P(),
        P(),
        P(),
        P(),
        P(None, "seq"),
        P(None, "seq"),
        P("seq", None),
        P("rep", "seq", None),
    )
    out_specs = (
        P("rep", "seq", None),
        P("rep", "seq", None),
        P("seq", None),
        P("seq", None),
        P(),
        P(),
        P(),
        P(),
        P(),
        P(None, "seq"),
        P(None, "seq"),
        P("seq", None),
    )
    return jax.shard_map(
        on_device, mesh=mesh, in_specs=in_specs, out_specs=out_specs, check_vma=False
    )
```

profile of v0, /device:TPU:0, one launch (start us, length us, event | category | flops | bytes accessed | tf_op | source)
XLA Modules:
  0.0 4016.5 jit_solution(8021908718773649853)
XLA Ops:
  9.3 132.8 %all-gather.5.cloned.1.call-done = bf16[1536,4608]{1,0:T(8,128)(2,1)} async-done(((bf16[192,4608]{1,0:T(8,128)(2,1)}), bf16[1536,4608]{1,0:T(8,128)(2,1)}) %all-gather.5.cloned.1.call-update) | async-done | bytes 14155792 | tf_op jit(solution)/shard_map/all_gather | solution.py:209
  178.6 39.8 collective-permute-done.1
  218.4 47.0 %collective-permute-done = bf16[256,3072]{1,0:T(8,128)(2,1)} collective-permute-done((bf16[256,3072]{1,0:T(8,128)(2,1)}, bf16[256,3072]{1,0:T(8,128)(2,1)}, u32[]{:S(2)}, u32[]{:S(2)}) %collective-permute-start) | collective-permute-done | bytes 1572896 | tf_op jit(solution)/shard_map/ppermute | solution.py:14
  286.9 341.3 %while.34 = (s32[]{:T(128)}, f32[8,256,2,96]{1,3,2,0:T(8,128)S(1)}, f32[8,2,256,1]{2,1,3,0:T(2,128)}, bf16[8,1024,2,96]{1,3,2,0:T(8,128)(2,1)}, f32[8,2,2]{2,1,0...) while((s32[]{:T(128)}, f32[8,256,2,96]{1,3,2,0:T(8,128)S(1)}, ...), condition=%wide.region_4.5_spmd.clone, body=%wide.region_1.4_spmd.clone.sunk | while | flops 281692032 | bytes 160720624 | solution.py:238
  291.5 34.6 select_reduce_fusion.2
  334.2 34.6 select_reduce_fusion.2
  376.8 34.6 select_reduce_fusion.2
  419.5 34.6 select_reduce_fusion.2
  462.1 34.6 select_reduce_fusion.2
  504.7 34.6 select_reduce_fusion.2
  547.4 34.6 select_reduce_fusion.2
  590.0 34.6 select_reduce_fusion.2
  652.1 102.0 %all-gather.9.cloned.1.call-done = bf16[2048,1536]{1,0:T(8,128)(2,1)} async-done(((bf16[256,1536]{1,0:T(8,128)(2,1)}), bf16[2048,1536]{1,0:T(8,128)(2,1)}) %all-gather.9.cloned.1.call-update) | async-done | bytes 6291472 | tf_op jit(solution)/shard_map/all_gather | solution.py:255
  767.9 51.8 %all-gather.11.cloned.1.call-done = bf16[2048,1536]{1,0:T(8,128)(2,1)} async-done(((bf16[256,1536]{1,0:T(8,128)(2,1)}), bf16[2048,1536]{1,0:T(8,128)(2,1)}) %all-gather.11.cloned.1.call-update) | async-done | bytes 6291472 | tf_op jit(solution)/shard_map/all_gather | solution.py:266
  848.9 61.1 %reduce-scatter.7.cloned.1.call-done = bf16[256,1536]{1,0:T(8,128)(2,1)} async-done(((bf16[2048,1536]{1,0:T(8,128)(2,1)}), bf16[256,1536]{1,0:T(8,128)(2,1)}) %reduce-scatter.7.cloned.1.call-update) | async-done | bytes 786448 | tf_op jit(solution)/shard_map/reduce_scatter | solution.py:280
  912.2 68.2 %reduce-scatter.5.cloned.1.call-done = bf16[256,1536]{1,0:T(8,128)(2,1)} async-done(((bf16[2048,1536]{1,0:T(8,128)(2,1)}), bf16[256,1536]{1,0:T(8,128)(2,1)}) %reduce-scatter.5.cloned.1.call-update) | async-done | bytes 786448 | tf_op jit(solution)/shard_map/reduce_scatter | solution.py:259
  1008.2 2550.7 %while.35 = (s32[]{:T(128)}, f32[8,261,2,96]{3,1,2,0:T(8,128)}, f32[8,1034,2,96]{1,3,2,0:T(8,128)}, f32[8,1024,2,96]{1,3,2,0:T(8,128)}, f32[8,2,6,11]{3,1,0,2:T(...) while((s32[]{:T(128)}, f32[8,261,2,96]{3,1,2,0:T(8,128)}, ...), condition=%wide.region_83.84_spmd.clone, body=%wide.region_13.83_spmd.clone.sunk | while | flops 1772737280 | bytes 370601792 | solution.py:304
  1041.3 36.7 multiply_reduce_fusion.77
  1078.0 11.8 multiply_reduce_fusion.78
  1163.3 124.6 %multiply_multiply_fusion.4 = f32[2,261,1034]{2,1,0:T(8,128)S(1)} fusion(f32[2,256,1024]{2,1,0:T(8,128)} %get-tuple-element.1464, f32[261,1034]{1,0:T(8,128)} %fusion.360, f32[2]{0:T(128)} %get-tuple-element.1396, f32[2]{0:T(128)} %get-tuple-element.1397, f32[2]{0:T(128)} %get-tuple-element.1398, f32[2]{0:T(128)} %get-tuple-element.1399, ...), kind=kLoop, calls=%fused_computation.436.clone.1 | loop fusion | flops 71786448 | bytes 5336168 | tf_op jit(solution)/shard_map/while/body/eval_jaxpr/mul | solution.py:121
  1356.6 36.7 multiply_reduce_fusion.77
  1393.3 11.8 multiply_reduce_fusion.78
  1478.6 124.6 %multiply_multiply_fusion.4 = f32[2,261,1034]{2,1,0:T(8,128)S(1)} fusion(f32[2,256,1024]{2,1,0:T(8,128)} %get-tuple-element.1464, f32[261,1034]{1,0:T(8,128)} %fusion.360, f32[2]{0:T(128)} %get-tuple-element.1396, f32[2]{0:T(128)} %get-tuple-element.1397, f32[2]{0:T(128)} %get-tuple-element.1398, f32[2]{0:T(128)} %get-tuple-element.1399, ...), kind=kLoop, calls=%fused_computation.436.clone.1 | loop fusion | flops 71786448 | bytes 5336168 | tf_op jit(solution)/shard_map/while/body/eval_jaxpr/mul | solution.py:121
  1671.8 36.7 multiply_reduce_fusion.77
  1708.5 11.8 multiply_reduce_fusion.78
  1772.0 11.3 multiply_reduce_fusion.81
  1793.8 124.6 %multiply_multiply_fusion.4 = f32[2,261,1034]{2,1,0:T(8,128)S(1)} fusion(f32[2,256,1024]{2,1,0:T(8,128)} %get-tuple-element.1464, f32[261,1034]{1,0:T(8,128)} %fusion.360, f32[2]{0:T(128)} %get-tuple-element.1396, f32[2]{0:T(128)} %get-tuple-element.1397, f32[2]{0:T(128)} %get-tuple-element.1398, f32[2]{0:T(128)} %get-tuple-element.1399, ...), kind=kLoop, calls=%fused_computation.436.clone.1 | loop fusion | flops 71786448 | bytes 5336168 | tf_op jit(solution)/shard_map/while/body/eval_jaxpr/mul | solution.py:121
  1987.1 36.7 multiply_reduce_fusion.77
  2023.8 11.8 multiply_reduce_fusion.78
  2109.1 124.6 %multiply_multiply_fusion.4 = f32[2,261,1034]{2,1,0:T(8,128)S(1)} fusion(f32[2,256,1024]{2,1,0:T(8,128)} %get-tuple-element.1464, f32[261,1034]{1,0:T(8,128)} %fusion.360, f32[2]{0:T(128)} %get-tuple-element.1396, f32[2]{0:T(128)} %get-tuple-element.1397, f32[2]{0:T(128)} %get-tuple-element.1398, f32[2]{0:T(128)} %get-tuple-element.1399, ...), kind=kLoop, calls=%fused_computation.436.clone.1 | loop fusion | flops 71786448 | bytes 5336168 | tf_op jit(solution)/shard_map/while/body/eval_jaxpr/mul | solution.py:121
  2302.4 36.7 multiply_reduce_fusion.77
  2339.1 11.8 multiply_reduce_fusion.78
  2424.4 124.6 %multiply_multiply_fusion.4 = f32[2,261,1034]{2,1,0:T(8,128)S(1)} fusion(f32[2,256,1024]{2,1,0:T(8,128)} %get-tuple-element.1464, f32[261,1034]{1,0:T(8,128)} %fusion.360, f32[2]{0:T(128)} %get-tuple-element.1396, f32[2]{0:T(128)} %get-tuple-element.1397, f32[2]{0:T(128)} %get-tuple-element.1398, f32[2]{0:T(128)} %get-tuple-element.1399, ...), kind=kLoop, calls=%fused_computation.436.clone.1 | loop fusion | flops 71786448 | bytes 5336168 | tf_op jit(solution)/shard_map/while/body/eval_jaxpr/mul | solution.py:121
  2617.6 36.7 multiply_reduce_fusion.77
  2654.3 11.8 multiply_reduce_fusion.78
  2739.6 124.6 %multiply_multiply_fusion.4 = f32[2,261,1034]{2,1,0:T(8,128)S(1)} fusion(f32[2,256,1024]{2,1,0:T(8,128)} %get-tuple-element.1464, f32[261,1034]{1,0:T(8,128)} %fusion.360, f32[2]{0:T(128)} %get-tuple-element.1396, f32[2]{0:T(128)} %get-tuple-element.1397, f32[2]{0:T(128)} %get-tuple-element.1398, f32[2]{0:T(128)} %get-tuple-element.1399, ...), kind=kLoop, calls=%fused_computation.436.clone.1 | loop fusion | flops 71786448 | bytes 5336168 | tf_op jit(solution)/shard_map/while/body/eval_jaxpr/mul | solution.py:121
  2932.9 36.7 multiply_reduce_fusion.77
  2969.6 11.8 multiply_reduce_fusion.78
  3054.9 124.6 %multiply_multiply_fusion.4 = f32[2,261,1034]{2,1,0:T(8,128)S(1)} fusion(f32[2,256,1024]{2,1,0:T(8,128)} %get-tuple-element.1464, f32[261,1034]{1,0:T(8,128)} %fusion.360, f32[2]{0:T(128)} %get-tuple-element.1396, f32[2]{0:T(128)} %get-tuple-element.1397, f32[2]{0:T(128)} %get-tuple-element.1398, f32[2]{0:T(128)} %get-tuple-element.1399, ...), kind=kLoop, calls=%fused_computation.436.clone.1 | loop fusion | flops 71786448 | bytes 5336168 | tf_op jit(solution)/shard_map/while/body/eval_jaxpr/mul | solution.py:121
  3248.2 36.7 multiply_reduce_fusion.77
  3284.9 11.8 multiply_reduce_fusion.78
  3370.2 124.6 %multiply_multiply_fusion.4 = f32[2,261,1034]{2,1,0:T(8,128)S(1)} fusion(f32[2,256,1024]{2,1,0:T(8,128)} %get-tuple-element.1464, f32[261,1034]{1,0:T(8,128)} %fusion.360, f32[2]{0:T(128)} %get-tuple-element.1396, f32[2]{0:T(128)} %get-tuple-element.1397, f32[2]{0:T(128)} %get-tuple-element.1398, f32[2]{0:T(128)} %get-tuple-element.1399, ...), kind=kLoop, calls=%fused_computation.436.clone.1 | loop fusion | flops 71786448 | bytes 5336168 | tf_op jit(solution)/shard_map/while/body/eval_jaxpr/mul | solution.py:121
  3591.8 28.7 collective-permute-done.7
  3620.5 38.8 collective-permute-done.6
  3693.2 147.7 %reduce-scatter.9.cloned.1.call-done = bf16[192,4608]{1,0:T(8,128)(2,1)} async-done(((bf16[1536,4608]{1,0:T(8,128)(2,1)}), bf16[192,4608]{1,0:T(8,128)(2,1)}) %reduce-scatter.9.cloned.1.call-update) | async-done | bytes 1769488 | tf_op jit(solution)/shard_map/reduce_scatter | solution.py:339
  3842.2 11.5 fusion.270
  3853.7 40.1 all-reduce.2
  3898.0 100.9 %all-reduce.6.cloned.1.call-done = (bf16[192,4608]{1,0:T(8,128)(2,1)}, bf16[192,1536]{1,0:T(8,128)(2,1)}, bf16[1536,512]{1,0:T(8,128)(2,1)}, bf16[1536,512]{1,0:T(8,128)(2,1)}, bf16[512,1536]{1,0:T(8,128)(2,1)}) async-done(((bf16[192,4608]{1,0:T(8,128)(2,1)}, bf16[192,1536]{1,0:T(8,128)(2,1)}, bf16[1536,512]{1,0:T(8,128)(2,1)}, bf16[1536,512]{1,0:T(8,128)(2,1)}, bf16[512,1536]{1,0:T(8,128)(2,1)}), ...) | async-done | bytes 7077904 | tf_op jit(solution)/shard_map/psum | solution.py:351
  (1975 shorter events, 1423.3 us)
Async XLA Ops:
  7.2 812.5 %copy-start = (bf16[512,1536]{1,0:T(8,128)(2,1)S(1)}, bf16[512,1536]{1,0:T(8,128)(2,1)}, u32[]{:S(2)}) copy-start(bf16[512,1536]{1,0:T(8,128)(2,1)} %param.30) | copy-start | bytes 4718596
  7.2 134.9 %copy-start.64 = (f32[1536]{0:T(1024)S(1)}, f32[1536]{0:T(1024)}, u32[]{:S(2)}) copy-start(f32[1536]{0:T(1024)} %param.25) | copy-start | bytes 18436
  7.2 134.8 %all-gather.5.cloned.1.call-start = ((), (), s32[]{:S(2)}) async-start(), calls=%async_computation.4 | async-start | bytes 15925248 | tf_op jit(solution)/shard_map/all_gather | solution.py:209
  8.0 634.8 %all-gather.7.cloned.1.call-start = ((), (), s32[]{:S(2)}) async-start(), calls=%async_computation.5 | async-start | bytes 5308416 | tf_op jit(solution)/shard_map/all_gather | solution.py:210
  9.3 142.0 %copy-start.72 = (f32[256]{0:T(256)}, f32[256]{0:T(256)S(1)}, u32[]{:S(2)}) copy-start(f32[256]{0:T(256)S(1)} %get-tuple-element.869) | copy-start | bytes 3076
  152.7 14.9 copy-start.77
  152.7 15.0 copy-start.70
  154.1 24.5 collective-permute-start.2
  157.4 61.1 %collective-permute-start.1 = (bf16[256,3072]{1,0:T(8,128)(2,1)}, bf16[256,3072]{1,0:T(8,128)(2,1)}, u32[]{:S(2)}, u32[]{:S(2)}) collective-permute-start(bf16[256,3072]{1,0:T(8,128)(2,1)} %slice.2477), channel_id=1, source_target_pairs={{0,2},{1,3},{2,4},{3,5},{4,6},{5,7},{8,10},{9,11},{10,12},{11,13},... | collective-permute-start | bytes 4718600 | tf_op jit(solution)/shard_map/ppermute | solution.py:14
  159.8 105.6 %collective-permute-start = (bf16[256,3072]{1,0:T(8,128)(2,1)}, bf16[256,3072]{1,0:T(8,128)(2,1)}, u32[]{:S(2)}, u32[]{:S(2)}) collective-permute-start(bf16[256,3072]{1,0:T(8,128)(2,1)} %slice.2477), channel_id=1, source_target_pairs={{0,3},{1,4},{2,5},{3,6},{4,7},{8,11},{9,12},{10,13},{11,14},{12,15... | collective-permute-start | bytes 4718600 | tf_op jit(solution)/shard_map/ppermute | solution.py:14
  162.3 591.8 %all-gather.9.cloned.1.call-start = ((), (), s32[]{:S(2)}) async-start(), calls=%async_computation.6 | async-start | bytes 7077888 | tf_op jit(solution)/shard_map/all_gather | solution.py:255
  165.4 3.6 collective-permute-start.3
  649.5 170.1 %all-gather.11.cloned.1.call-start = ((), (), s32[]{:S(2)}) async-start(), calls=%async_computation.8 | async-start | bytes 7077888 | tf_op jit(solution)/shard_map/all_gather | solution.py:266
  651.8 258.2 %reduce-scatter.7.cloned.1.call-start = ((), (), s32[]{:S(2)}) async-start(), calls=%async_computation.9 | async-start | bytes 7077888 | tf_op jit(solution)/shard_map/reduce_scatter | solution.py:280
  841.4 139.0 %reduce-scatter.5.cloned.1.call-start = ((), (), s32[]{:S(2)}) async-start(), calls=%async_computation.7 | async-start | bytes 7077888 | tf_op jit(solution)/shard_map/reduce_scatter | solution.py:259
  848.4 61.6 %copy-start.12 = (f32[256,1536]{1,0:T(8,128)S(1)}, f32[256,1536]{1,0:T(8,128)}, u32[]{:S(2)}) copy-start(f32[256,1536]{1,0:T(8,128)} %copy-done.11) | copy-start | bytes 4718596
  848.4 2844.7 %reduce-scatter.11.cloned.1.call-start = ((), (), s32[]{:S(2)}) async-start(), calls=%async_computation.11 | async-start | bytes 5308416 | tf_op jit(solution)/shard_map/reduce_scatter | solution.py:342
  1008.2 2832.7 %reduce-scatter.9.cloned.1.call-start = ((), (), s32[]{:S(2)}) async-start(), calls=%async_computation.10 | async-start | bytes 15925248 | tf_op jit(solution)/shard_map/reduce_scatter | solution.py:339
  1141.5 11.3 copy-start.2
  1287.9 50.7 %copy-start.68 = (f32[2]{0:T(128)S(1)}, f32[2]{0:T(128)}, u32[]{:S(2)}) copy-start(f32[2]{0:T(128)} %get-tuple-element.1468) | copy-start | bytes 28 | tf_op jit(solution)/shard_map/while
  1287.9 50.7 %copy-start.69 = (f32[2]{0:T(128)S(1)}, f32[2]{0:T(128)}, u32[]{:S(2)}) copy-start(f32[2]{0:T(128)} %get-tuple-element.1466) | copy-start | bytes 28 | tf_op jit(solution)/shard_map/while
  1456.8 11.3 copy-start.2
  1603.2 50.7 %copy-start.68 = (f32[2]{0:T(128)S(1)}, f32[2]{0:T(128)}, u32[]{:S(2)}) copy-start(f32[2]{0:T(128)} %get-tuple-element.1468) | copy-start | bytes 28 | tf_op jit(solution)/shard_map/while
  1603.2 50.7 %copy-start.69 = (f32[2]{0:T(128)S(1)}, f32[2]{0:T(128)}, u32[]{:S(2)}) copy-start(f32[2]{0:T(128)} %get-tuple-element.1466) | copy-start | bytes 28 | tf_op jit(solution)/shard_map/while
  1918.5 50.7 %copy-start.68 = (f32[2]{0:T(128)S(1)}, f32[2]{0:T(128)}, u32[]{:S(2)}) copy-start(f32[2]{0:T(128)} %get-tuple-element.1468) | copy-start | bytes 28 | tf_op jit(solution)/shard_map/while
  1918.5 50.7 %copy-start.69 = (f32[2]{0:T(128)S(1)}, f32[2]{0:T(128)}, u32[]{:S(2)}) copy-start(f32[2]{0:T(128)} %get-tuple-element.1466) | copy-start | bytes 28 | tf_op jit(solution)/shard_map/while
  2233.7 50.7 %copy-start.68 = (f32[2]{0:T(128)S(1)}, f32[2]{0:T(128)}, u32[]{:S(2)}) copy-start(f32[2]{0:T(128)} %get-tuple-element.1468) | copy-start | bytes 28 | tf_op jit(solution)/shard_map/while
  2233.7 50.7 %copy-start.69 = (f32[2]{0:T(128)S(1)}, f32[2]{0:T(128)}, u32[]{:S(2)}) copy-start(f32[2]{0:T(128)} %get-tuple-element.1466) | copy-start | bytes 28 | tf_op jit(solution)/shard_map/while
  2549.0 50.7 %copy-start.68 = (f32[2]{0:T(128)S(1)}, f32[2]{0:T(128)}, u32[]{:S(2)}) copy-start(f32[2]{0:T(128)} %get-tuple-element.1468) | copy-start | bytes 28 | tf_op jit(solution)/shard_map/while
  2549.0 50.7 %copy-start.69 = (f32[2]{0:T(128)S(1)}, f32[2]{0:T(128)}, u32[]{:S(2)}) copy-start(f32[2]{0:T(128)} %get-tuple-element.1466) | copy-start | bytes 28 | tf_op jit(solution)/shard_map/while
  2864.2 50.7 %copy-start.68 = (f32[2]{0:T(128)S(1)}, f32[2]{0:T(128)}, u32[]{:S(2)}) copy-start(f32[2]{0:T(128)} %get-tuple-element.1468) | copy-start | bytes 28 | tf_op jit(solution)/shard_map/while
  2864.2 50.7 %copy-start.69 = (f32[2]{0:T(128)S(1)}, f32[2]{0:T(128)}, u32[]{:S(2)}) copy-start(f32[2]{0:T(128)} %get-tuple-element.1466) | copy-start | bytes 28 | tf_op jit(solution)/shard_map/while
  3179.5 50.7 %copy-start.68 = (f32[2]{0:T(128)S(1)}, f32[2]{0:T(128)}, u32[]{:S(2)}) copy-start(f32[2]{0:T(128)} %get-tuple-element.1468) | copy-start | bytes 28 | tf_op jit(solution)/shard_map/while
  3179.5 50.7 %copy-start.69 = (f32[2]{0:T(128)S(1)}, f32[2]{0:T(128)}, u32[]{:S(2)}) copy-start(f32[2]{0:T(128)} %get-tuple-element.1466) | copy-start | bytes 28 | tf_op jit(solution)/shard_map/while
  3494.8 50.7 %copy-start.68 = (f32[2]{0:T(128)S(1)}, f32[2]{0:T(128)}, u32[]{:S(2)}) copy-start(f32[2]{0:T(128)} %get-tuple-element.1468) | copy-start | bytes 28 | tf_op jit(solution)/shard_map/while
  3494.8 50.7 %copy-start.69 = (f32[2]{0:T(128)S(1)}, f32[2]{0:T(128)}, u32[]{:S(2)}) copy-start(f32[2]{0:T(128)} %get-tuple-element.1466) | copy-start | bytes 28 | tf_op jit(solution)/shard_map/while
  3579.2 12.6 collective-permute-start.5
  3580.5 40.1 collective-permute-start.7
  3581.8 77.6 %collective-permute-start.6 = (bf16[256,3072]{0,1:T(8,128)(2,1)}, bf16[256,3072]{0,1:T(8,128)(2,1)}, u32[]{:S(2)}, u32[]{:S(2)}) collective-permute-start(bf16[256,3072]{0,1:T(8,128)(2,1)} %get-tuple-element.859), channel_id=1, source_target_pairs={{2,0},{3,1},{4,2},{5,3},{6,4},{7,5},{10,8},{11,9},{12,10},{13,11},... | collective-permute-start | bytes 4718600 | tf_op jit(solution)/shard_map/ppermute | solution.py:14
  3587.7 3.8 collective-permute-start.4
  3591.7 71.6 %copy-start.15 = (bf16[1,256,1536]{2,1,0:T(8,128)(2,1)S(1)}, bf16[1,256,1536]{2,1,0:T(8,128)(2,1)}, u32[]{:S(2)}) copy-start(bf16[1,256,1536]{2,1,0:T(8,128)(2,1)} %param.18) | copy-start | bytes 2359300
  3591.8 71.5 %copy-start.20 = (bf16[251,8,2,96]{0,3,2,1:T(8,128)(2,1)S(1)}, bf16[251,8,2,96]{0,3,2,1:T(8,128)(2,1)}, u32[]{:S(2)}) copy-start(bf16[251,8,2,96]{0,3,2,1:T(8,128)(2,1)} %slice.3701) | copy-start | bytes 2313220
  3591.8 71.5 %copy-start.65 = (f32[1536]{0:T(1024)S(1)}, f32[1536]{0:T(1024)}, u32[]{:S(2)}) copy-start(f32[1536]{0:T(1024)} %param.25) | copy-start | bytes 18436
  3591.8 71.5 %copy-start.73 = (f32[256]{0:T(256)S(1)}, f32[256]{0:T(256)}, u32[]{:S(2)}) copy-start(f32[256]{0:T(256)} %copy-done.72) | copy-start | bytes 3076
  3672.5 326.4 %all-reduce.6.cloned.1.call-start = ((), (), s32[]{:S(2)}) async-start(), calls=%async_computation.12 | async-start | bytes 14155776 | tf_op jit(solution)/shard_map/psum | solution.py:351
  3672.6 16.0 slice-start.1
  3842.2 11.5 copy-start.71
  3842.2 53.1 %copy-start.8 = (f32[256,1536]{1,0:T(8,128)S(1)}, f32[256,1536]{1,0:T(8,128)}, u32[]{:S(2)}) copy-start(f32[256,1536]{1,0:T(8,128)} %copy-done.7) | copy-start | bytes 4718596
  (393 other events, 3093.1 us)
Sparse Core Ops, SparseCore 0:
  9.7 132.3 all-gather.4
  162.4 82.5 all-gather.6
  649.7 104.4 all-gather.8
  756.2 63.4 all-gather.10
  841.5 68.4 reduce-scatter.6
  912.1 68.1 reduce-scatter.4
  1008.3 53.3 reduce-scatter.10
  3672.7 168.1 reduce-scatter.8
  3846.3 152.5 all-reduce.5
where the time goes:
time: 4040 us; the launch traced here: 4020 us
  other arithmetic  2010 us (50%)
  local copies, waits for them, and re-layouts  853 us (21%)
  waiting for transfers between devices  821 us (20%)
  matrix products  225 us (6%)
    mul x8, other arithmetic, attend_group_back(): dlogits = convolve_back(dconv, kernel_g) * mask_ext * score_scale  997 us
    another operation x576, local copies, waits for them, and re-layouts, kernel_grads(): entries.append(jnp.stack(line_sums, axis=-1))  678 us
    reduce_sum x32, other arithmetic, kernel_grads(): line_sums.append(jnp.sum(grads * window_part, axis=(1, 2)))  334 us
    reduce_sum x8, other arithmetic, attend_group_back(): dconv = prob * (dprob - jnp.sum(prob * dprob, axis=-1, keepdims=True))  294 us
    reduce_max x8, other arithmetic, attend_group(): peak = jnp.max(jnp.where(allowed, conv, -1e+30), axis=-1, keepdims=True)  277 us
    ppermute x8, waiting for transfers between devices, from_behind(): return lax.ppermute(x, axis, pairs)  155 us
    reduce_scatter x1, waiting for transfers between devices, on_device(): lax.psum_scatter(whole_input_grad.astype(jnp.bfloat16), 'seq', scatter_di...  148 us
    all_gather x1, waiting for transfers between devices, on_device(): lax.all_gather(input_weight, 'seq', axis=0, tiled=True)  133 us
  transfers between devices with their start and end apart: 17, of which 12 were waited for; matrix products, arithmetic and copies ran while one was open for 74% of the time, Pallas kernels for 0%

commit v1 on v0

--- a/solution.py
+++ b/solution.py
@@ -1,3 +1,4 @@
+import functools
 import jax
 import jax.numpy as jnp
 from jax import lax
@@ -6,6 +7,21 @@
 REACH = 4
 EPS = 1e-06
 HIGHEST = lax.Precision.HIGHEST
+
+
+def table_use(original, axis_key, d_out):
+    r2, prior, upper = (lax.axis_size(axis_key), lax.axis_index(axis_key), original.shape[d_out])
+    extra, frame_out = (original, 1)
+    while frame_out < r2:
+        extra = jnp.concatenate(
+            [extra, lax.ppermute(extra, axis_key, [(m, (m - frame_out) % r2) for m in range(r2)])],
+            d_out,
+        )
+        frame_out = 2 * frame_out
+    return jnp.roll(extra, prior * upper, d_out)
+
+
+stacks_all_tell = functools.partial(table_use, axis_key="seq", d_out=0)
 
 
 def from_behind(x, axis, by):
@@ -252,7 +268,7 @@
     normed_mid = (resid * second_scale * second_gain).astype(jnp.bfloat16)
     dmlp = (row_valid * grad_out).astype(jnp.bfloat16)
     contract_rows = (((0,), (0,)), ((), ()))
-    inputs_all = lax.all_gather(normed_mid, "seq", axis=0, tiled=True)
+    inputs_all = stacks_all_tell(normed_mid)
     gate = jnp.dot(inputs_all, gate_weight, preferred_element_type=jnp.float32)
     up_proj = jnp.dot(inputs_all, up_weight, preferred_element_type=jnp.float32)
     hidden = (jax.nn.silu(gate) * up_proj).astype(jnp.bfloat16)

time: 4040 us -> 3090 us (0.76)
  other arithmetic: 2010 us -> 1370 us
  local copies, waits for them, and re-layouts: 853 us -> 441 us
  waiting for transfers between devices: 821 us -> 893 us
    mul x8, other arithmetic: 997 us -> 356 us  [attend_group_back(): dlogits = convolve_back(dconv, kernel_g) * mask_ext * score_scale]
    another operation x576, local copies, waits for them, and re-layouts: 678 us -> 235 us  [kernel_grads(): entries.append(jnp.stack(line_sums, axis=-1))]
    ppermute x0 -> x3, waiting for transfers between devices: none -> 210 us  [table_use(): lax.ppermute(extra, axis_key, [(m, (m - frame_out) % r2) for m in range(r...]
    all_gather x1 -> x0, waiting for transfers between devices: 102 us -> none  [on_device(): inputs_all = lax.all_gather(normed_mid, 'seq', axis=0, tiled=True)]
    all_gather x1, waiting for transfers between devices: 51.8 us -> 0.01 us  [on_device(): dmlp_all = lax.all_gather(dmlp, 'seq', axis=0, tiled=True)]
  transfers between devices with their start and end apart: 17 -> 19, of which waited for: 12 -> 13; matrix products, arithmetic and copies ran while one was open for 74% -> 64% of each run, Pallas kernels for 0% -> 0%
where the time goes in v1:
time: 3090 us; the launch traced here: 3070 us
  other arithmetic  1370 us (44%)
  waiting for transfers between devices  893 us (29%)
  local copies, waits for them, and re-layouts  441 us (14%)
  matrix products  249 us (8%)
  starting transfers between devices  46.1 us (1%)
  blocking collectives  40.1 us (1%)
    mul x8, other arithmetic, attend_group_back(): dlogits = convolve_back(dconv, kernel_g) * mask_ext * score_scale  356 us
    reduce_sum x32, other arithmetic, kernel_grads(): line_sums.append(jnp.sum(grads * window_part, axis=(1, 2)))  335 us
    reduce_sum x8, other arithmetic, attend_group_back(): dconv = prob * (dprob - jnp.sum(prob * dprob, axis=-1, keepdims=True))  294 us
    reduce_max x8, other arithmetic, attend_group(): peak = jnp.max(jnp.where(allowed, conv, -1e+30), axis=-1, keepdims=True)  277 us
    another operation x576, local copies, waits for them, and re-layouts, kernel_grads(): entries.append(jnp.stack(line_sums, axis=-1))  235 us
    ppermute x3, waiting for transfers between devices, table_use(): lax.ppermute(extra, axis_key, [(m, (m - frame_out) % r2) for m in range(r...  210 us
    ppermute x8, waiting for transfers between devices, from_behind(): return lax.ppermute(x, axis, pairs)  176 us
    reduce_scatter x1, waiting for transfers between devices, on_device(): lax.psum_scatter(whole_input_grad.astype(jnp.bfloat16), 'seq', scatter_di...  139 us
  transfers between devices with their start and end apart: 19, of which 13 were waited for; matrix products, arithmetic and copies ran while one was open for 64% of the time, Pallas kernels for 0%

profile of v1, /device:TPU:0, one launch (start us, length us, event | category | flops | bytes accessed | tf_op | source)
XLA Modules:
  0.0 3073.3 jit_solution(1893872459746331300)
XLA Ops:
  9.7 132.4 %all-gather.4.cloned.1.call-done = bf16[1536,4608]{1,0:T(8,128)(2,1)} async-done(((bf16[192,4608]{1,0:T(8,128)(2,1)}), bf16[1536,4608]{1,0:T(8,128)(2,1)}) %all-gather.4.cloned.1.call-update) | async-done | bytes 14155792 | tf_op jit(solution)/shard_map/all_gather | solution.py:225
  175.4 46.4 %collective-permute-done = bf16[256,3072]{1,0:T(8,128)(2,1)} collective-permute-done((bf16[256,3072]{1,0:T(8,128)(2,1)}, bf16[256,3072]{1,0:T(8,128)(2,1)}, u32[]{:S(2)}, u32[]{:S(2)}) %collective-permute-start) | collective-permute-done | bytes 1572896 | tf_op jit(solution)/shard_map/ppermute | solution.py:30
  221.8 54.2 %collective-permute-done.1 = bf16[256,3072]{1,0:T(8,128)(2,1)} collective-permute-done((bf16[256,3072]{1,0:T(8,128)(2,1)}, bf16[256,3072]{1,0:T(8,128)(2,1)}, u32[]{:S(2)}, u32[]{:S(2)}) %collective-permute-start.1) | collective-permute-done | bytes 1572896 | tf_op jit(solution)/shard_map/ppermute | solution.py:30
  297.7 337.3 %while.34 = (s32[]{:T(128)}, f32[8,256,2,96]{1,3,2,0:T(8,128)}, f32[8,2,256,1]{2,1,3,0:T(2,128)}, bf16[8,1024,2,96]{1,3,2,0:T(8,128)(2,1)}, f32[8,2,2]{2,1,0:T(2...) while((s32[]{:T(128)}, f32[8,256,2,96]{1,3,2,0:T(8,128)}, ...), condition=%wide.region_4.5_spmd.clone, body=%wide.region_1.4_spmd.clone.sunk | while | flops 281692032 | bytes 160720112 | solution.py:254
  300.7 34.6 %select_reduce_fusion.2 = (f32[2,256]{1,0:T(2,128)S(1)}, f32[2,256,1024]{2,1,0:T(8,128)S(1)}) fusion(pred[256,1024]{1,0:T(8,128)(4,1)S(1)} %broadcast_compare_fusion.5, f32[2,261,1034]{2,1,0:T(8,128)S(1)} %convolution_multiply_fusion.5, f32[2]{0:T(128)S(1)} %get-tuple-element.1302, f32[2]{0:T(128)S(1)} %get-tuple-element.1303, ...), kind=kLoop, calls=%fused_computation.136.clone.1 | loop fusion | flops 69729792 | bytes 140773904 | tf_op jit(solution)/shard_map/while/body/eval_jaxpr/reduce_max | solution.py:95
  342.8 34.6 %select_reduce_fusion.2 = (f32[2,256]{1,0:T(2,128)S(1)}, f32[2,256,1024]{2,1,0:T(8,128)S(1)}) fusion(pred[256,1024]{1,0:T(8,128)(4,1)S(1)} %broadcast_compare_fusion.5, f32[2,261,1034]{2,1,0:T(8,128)S(1)} %convolution_multiply_fusion.5, f32[2]{0:T(128)S(1)} %get-tuple-element.1302, f32[2]{0:T(128)S(1)} %get-tuple-element.1303, ...), kind=kLoop, calls=%fused_computation.136.clone.1 | loop fusion | flops 69729792 | bytes 140773904 | tf_op jit(solution)/shard_map/while/body/eval_jaxpr/reduce_max | solution.py:95
  384.9 34.6 %select_reduce_fusion.2 = (f32[2,256]{1,0:T(2,128)S(1)}, f32[2,256,1024]{2,1,0:T(8,128)S(1)}) fusion(pred[256,1024]{1,0:T(8,128)(4,1)S(1)} %broadcast_compare_fusion.5, f32[2,261,1034]{2,1,0:T(8,128)S(1)} %convolution_multiply_fusion.5, f32[2]{0:T(128)S(1)} %get-tuple-element.1302, f32[2]{0:T(128)S(1)} %get-tuple-element.1303, ...), kind=kLoop, calls=%fused_computation.136.clone.1 | loop fusion | flops 69729792 | bytes 140773904 | tf_op jit(solution)/shard_map/while/body/eval_jaxpr/reduce_max | solution.py:95
  427.1 34.6 %select_reduce_fusion.2 = (f32[2,256]{1,0:T(2,128)S(1)}, f32[2,256,1024]{2,1,0:T(8,128)S(1)}) fusion(pred[256,1024]{1,0:T(8,128)(4,1)S(1)} %broadcast_compare_fusion.5, f32[2,261,1034]{2,1,0:T(8,128)S(1)} %convolution_multiply_fusion.5, f32[2]{0:T(128)S(1)} %get-tuple-element.1302, f32[2]{0:T(128)S(1)} %get-tuple-element.1303, ...), kind=kLoop, calls=%fused_computation.136.clone.1 | loop fusion | flops 69729792 | bytes 140773904 | tf_op jit(solution)/shard_map/while/body/eval_jaxpr/reduce_max | solution.py:95
  469.2 34.6 %select_reduce_fusion.2 = (f32[2,256]{1,0:T(2,128)S(1)}, f32[2,256,1024]{2,1,0:T(8,128)S(1)}) fusion(pred[256,1024]{1,0:T(8,128)(4,1)S(1)} %broadcast_compare_fusion.5, f32[2,261,1034]{2,1,0:T(8,128)S(1)} %convolution_multiply_fusion.5, f32[2]{0:T(128)S(1)} %get-tuple-element.1302, f32[2]{0:T(128)S(1)} %get-tuple-element.1303, ...), kind=kLoop, calls=%fused_computation.136.clone.1 | loop fusion | flops 69729792 | bytes 140773904 | tf_op jit(solution)/shard_map/while/body/eval_jaxpr/reduce_max | solution.py:95
  511.4 34.6 %select_reduce_fusion.2 = (f32[2,256]{1,0:T(2,128)S(1)}, f32[2,256,1024]{2,1,0:T(8,128)S(1)}) fusion(pred[256,1024]{1,0:T(8,128)(4,1)S(1)} %broadcast_compare_fusion.5, f32[2,261,1034]{2,1,0:T(8,128)S(1)} %convolution_multiply_fusion.5, f32[2]{0:T(128)S(1)} %get-tuple-element.1302, f32[2]{0:T(128)S(1)} %get-tuple-element.1303, ...), kind=kLoop, calls=%fused_computation.136.clone.1 | loop fusion | flops 69729792 | bytes 140773904 | tf_op jit(solution)/shard_map/while/body/eval_jaxpr/reduce_max | solution.py:95
  553.5 34.6 %select_reduce_fusion.2 = (f32[2,256]{1,0:T(2,128)S(1)}, f32[2,256,1024]{2,1,0:T(8,128)S(1)}) fusion(pred[256,1024]{1,0:T(8,128)(4,1)S(1)} %broadcast_compare_fusion.5, f32[2,261,1034]{2,1,0:T(8,128)S(1)} %convolution_multiply_fusion.5, f32[2]{0:T(128)S(1)} %get-tuple-element.1302, f32[2]{0:T(128)S(1)} %get-tuple-element.1303, ...), kind=kLoop, calls=%fused_computation.136.clone.1 | loop fusion | flops 69729792 | bytes 140773904 | tf_op jit(solution)/shard_map/while/body/eval_jaxpr/reduce_max | solution.py:95
  595.6 34.6 %select_reduce_fusion.2 = (f32[2,256]{1,0:T(2,128)S(1)}, f32[2,256,1024]{2,1,0:T(8,128)S(1)}) fusion(pred[256,1024]{1,0:T(8,128)(4,1)S(1)} %broadcast_compare_fusion.5, f32[2,261,1034]{2,1,0:T(8,128)S(1)} %convolution_multiply_fusion.5, f32[2]{0:T(128)S(1)} %get-tuple-element.1302, f32[2]{0:T(128)S(1)} %get-tuple-element.1303, ...), kind=kLoop, calls=%fused_computation.136.clone.1 | loop fusion | flops 69729792 | bytes 140773904 | tf_op jit(solution)/shard_map/while/body/eval_jaxpr/reduce_max | solution.py:95
  660.1 53.8 %collective-permute-done.4 = bf16[256,1536]{1,0:T(8,128)(2,1)S(1)} collective-permute-done((bf16[256,1536]{1,0:T(8,128)(2,1)S(1)}, bf16[256,1536]{1,0:T(8,128)(2,1)S(1)}, u32[]{:S(2)}, u32[]{:S(2)}) %collective-permute-start.4) | collective-permute-done | bytes 786464 | tf_op jit(solution)/shard_map/ppermute | solution.py:17
  726.2 32.3 %collective-permute-done.5 = bf16[512,1536]{1,0:T(8,128)(2,1)S(1)} collective-permute-done((bf16[512,1536]{1,0:T(8,128)(2,1)S(1)}, bf16[512,1536]{1,0:T(8,128)(2,1)S(1)}, u32[]{:S(2)}, u32[]{:S(2)}) %collective-permute-start.5) | collective-permute-done | bytes 1572896 | tf_op jit(solution)/shard_map/ppermute | solution.py:17
  760.7 16.8 collective-permute-start.6
  789.2 124.2 %collective-permute-done.6 = bf16[1024,1536]{1,0:T(8,128)(2,1)} collective-permute-done((bf16[1024,1536]{1,0:T(8,128)(2,1)}, bf16[1024,1536]{1,0:T(8,128)(2,1)}, u32[]{:S(2)}, u32[]{:S(2)}) %collective-permute-start.6) | collective-permute-done | bytes 3145760 | tf_op jit(solution)/shard_map/ppermute | solution.py:17
  965.1 62.6 %reduce-scatter.7.cloned.1.call-done = bf16[256,1536]{1,0:T(8,128)(2,1)} async-done(((bf16[2048,1536]{1,0:T(8,128)(2,1)}), bf16[256,1536]{1,0:T(8,128)(2,1)}) %reduce-scatter.7.cloned.1.call-update) | async-done | bytes 786448 | tf_op jit(solution)/shard_map/reduce_scatter | solution.py:296
  1029.9 68.2 %reduce-scatter.5.cloned.1.call-done = bf16[256,1536]{1,0:T(8,128)(2,1)} async-done(((bf16[2048,1536]{1,0:T(8,128)(2,1)}), bf16[256,1536]{1,0:T(8,128)(2,1)}) %reduce-scatter.5.cloned.1.call-update) | async-done | bytes 786448 | tf_op jit(solution)/shard_map/reduce_scatter | solution.py:275
  1126.5 1489.3 %while.35 = (s32[]{:T(128)}, f32[8,261,2,96]{3,1,2,0:T(8,128)}, f32[8,1034,2,96]{1,3,2,0:T(8,128)}, f32[8,1024,2,96]{1,3,2,0:T(8,128)}, f32[8,2,6,11]{3,1,0,2:T(...) while((s32[]{:T(128)}, f32[8,261,2,96]{3,1,2,0:T(8,128)}, ...), condition=%wide.region_83.84_spmd.clone, body=%wide.region_13.83_spmd.clone.sunk | while | flops 1772737280 | bytes 377415552 | solution.py:320
  1137.6 36.7 %multiply_reduce_fusion.77 = (f32[2,256]{1,0:T(2,128)S(1)}, f32[2,256,1024]{2,1,0:T(8,128)S(1)}) fusion(f32[256,1024]{1,0:T(8,128)} %get-tuple-element.1394, f32[2]{0:T(128)} %get-tuple-element.1395, f32[256,1024]{1,0:T(8,128)S(1)} %get-tuple-element.1396, f32[2]{0:T(128)} %get-tuple-element.1397, f32[2,256]{1,0:T(2,128)S(1)} %fusion.372, ...), kind=kLoop, calls=%fused_computation.507.clone.1 | loop fusion | flops 72351232 | bytes 142873120 | tf_op jit(solution)/shard_map/while/body/eval_jaxpr/reduce_sum | solution.py:135
  1180.0 12.2 multiply_reduce_fusion.78
  1260.2 44.5 %multiply_multiply_fusion.4 = f32[2,261,1034]{2,1,0:T(8,128)} fusion(f32[2,256,1024]{2,1,0:T(8,128)S(1)} %copy-done.2, f32[261,1034]{1,0:T(8,128)} %fusion.373, f32[2]{0:T(128)S(1)} %get-tuple-element.1398, f32[2]{0:T(128)S(1)} %get-tuple-element.1399, f32[2]{0:T(128)S(1)} %get-tuple-element.1400, f32[2]{0:T(128)S(1)} %get-tuple-element.1401, ...), kind=kLoop, calls=%fused_computation.436.clone.1 | loop fusion | flops 71786448 | bytes 5336168 | tf_op jit(solution)/shard_map/while/body/eval_jaxpr/mul | solution.py:137
  1322.8 36.7 %multiply_reduce_fusion.77 = (f32[2,256]{1,0:T(2,128)S(1)}, f32[2,256,1024]{2,1,0:T(8,128)S(1)}) fusion(f32[256,1024]{1,0:T(8,128)} %get-tuple-element.1394, f32[2]{0:T(128)} %get-tuple-element.1395, f32[256,1024]{1,0:T(8,128)S(1)} %get-tuple-element.1396, f32[2]{0:T(128)} %get-tuple-element.1397, f32[2,256]{1,0:T(2,128)S(1)} %fusion.372, ...), kind=kLoop, calls=%fused_computation.507.clone.1 | loop fusion | flops 72351232 | bytes 142873120 | tf_op jit(solution)/shard_map/while/body/eval_jaxpr/reduce_sum | solution.py:135
  1365.2 12.2 multiply_reduce_fusion.78
  1445.3 44.5 %multiply_multiply_fusion.4 = f32[2,261,1034]{2,1,0:T(8,128)} fusion(f32[2,256,1024]{2,1,0:T(8,128)S(1)} %copy-done.2, f32[261,1034]{1,0:T(8,128)} %fusion.373, f32[2]{0:T(128)S(1)} %get-tuple-element.1398, f32[2]{0:T(128)S(1)} %get-tuple-element.1399, f32[2]{0:T(128)S(1)} %get-tuple-element.1400, f32[2]{0:T(128)S(1)} %get-tuple-element.1401, ...), kind=kLoop, calls=%fused_computation.436.clone.1 | loop fusion | flops 71786448 | bytes 5336168 | tf_op jit(solution)/shard_map/while/body/eval_jaxpr/mul | solution.py:137
  1508.0 36.7 %multiply_reduce_fusion.77 = (f32[2,256]{1,0:T(2,128)S(1)}, f32[2,256,1024]{2,1,0:T(8,128)S(1)}) fusion(f32[256,1024]{1,0:T(8,128)} %get-tuple-element.1394, f32[2]{0:T(128)} %get-tuple-element.1395, f32[256,1024]{1,0:T(8,128)S(1)} %get-tuple-element.1396, f32[2]{0:T(128)} %get-tuple-element.1397, f32[2,256]{1,0:T(2,128)S(1)} %fusion.372, ...), kind=kLoop, calls=%fused_computation.507.clone.1 | loop fusion | flops 72351232 | bytes 142873120 | tf_op jit(solution)/shard_map/while/body/eval_jaxpr/reduce_sum | solution.py:135
  1550.4 12.2 multiply_reduce_fusion.78
  1630.5 44.5 %multiply_multiply_fusion.4 = f32[2,261,1034]{2,1,0:T(8,128)} fusion(f32[2,256,1024]{2,1,0:T(8,128)S(1)} %copy-done.2, f32[261,1034]{1,0:T(8,128)} %fusion.373, f32[2]{0:T(128)S(1)} %get-tuple-element.1398, f32[2]{0:T(128)S(1)} %get-tuple-element.1399, f32[2]{0:T(128)S(1)} %get-tuple-element.1400, f32[2]{0:T(128)S(1)} %get-tuple-element.1401, ...), kind=kLoop, calls=%fused_computation.436.clone.1 | loop fusion | flops 71786448 | bytes 5336168 | tf_op jit(solution)/shard_map/while/body/eval_jaxpr/mul | solution.py:137
  1693.2 36.7 %multiply_reduce_fusion.77 = (f32[2,256]{1,0:T(2,128)S(1)}, f32[2,256,1024]{2,1,0:T(8,128)S(1)}) fusion(f32[256,1024]{1,0:T(8,128)} %get-tuple-element.1394, f32[2]{0:T(128)} %get-tuple-element.1395, f32[256,1024]{1,0:T(8,128)S(1)} %get-tuple-element.1396, f32[2]{0:T(128)} %get-tuple-element.1397, f32[2,256]{1,0:T(2,128)S(1)} %fusion.372, ...), kind=kLoop, calls=%fused_computation.507.clone.1 | loop fusion | flops 72351232 | bytes 142873120 | tf_op jit(solution)/shard_map/while/body/eval_jaxpr/reduce_sum | solution.py:135
  1735.6 12.2 multiply_reduce_fusion.78
  1815.7 44.5 %multiply_multiply_fusion.4 = f32[2,261,1034]{2,1,0:T(8,128)} fusion(f32[2,256,1024]{2,1,0:T(8,128)S(1)} %copy-done.2, f32[261,1034]{1,0:T(8,128)} %fusion.373, f32[2]{0:T(128)S(1)} %get-tuple-element.1398, f32[2]{0:T(128)S(1)} %get-tuple-element.1399, f32[2]{0:T(128)S(1)} %get-tuple-element.1400, f32[2]{0:T(128)S(1)} %get-tuple-element.1401, ...), kind=kLoop, calls=%fused_computation.436.clone.1 | loop fusion | flops 71786448 | bytes 5336168 | tf_op jit(solution)/shard_map/while/body/eval_jaxpr/mul | solution.py:137
  1878.3 36.7 %multiply_reduce_fusion.77 = (f32[2,256]{1,0:T(2,128)S(1)}, f32[2,256,1024]{2,1,0:T(8,128)S(1)}) fusion(f32[256,1024]{1,0:T(8,128)} %get-tuple-element.1394, f32[2]{0:T(128)} %get-tuple-element.1395, f32[256,1024]{1,0:T(8,128)S(1)} %get-tuple-element.1396, f32[2]{0:T(128)} %get-tuple-element.1397, f32[2,256]{1,0:T(2,128)S(1)} %fusion.372, ...), kind=kLoop, calls=%fused_computation.507.clone.1 | loop fusion | flops 72351232 | bytes 142873120 | tf_op jit(solution)/shard_map/while/body/eval_jaxpr/reduce_sum | solution.py:135
  1920.7 12.2 multiply_reduce_fusion.78
  2000.9 44.5 %multiply_multiply_fusion.4 = f32[2,261,1034]{2,1,0:T(8,128)} fusion(f32[2,256,1024]{2,1,0:T(8,128)S(1)} %copy-done.2, f32[261,1034]{1,0:T(8,128)} %fusion.373, f32[2]{0:T(128)S(1)} %get-tuple-element.1398, f32[2]{0:T(128)S(1)} %get-tuple-element.1399, f32[2]{0:T(128)S(1)} %get-tuple-element.1400, f32[2]{0:T(128)S(1)} %get-tuple-element.1401, ...), kind=kLoop, calls=%fused_computation.436.clone.1 | loop fusion | flops 71786448 | bytes 5336168 | tf_op jit(solution)/shard_map/while/body/eval_jaxpr/mul | solution.py:137
  2063.5 36.7 %multiply_reduce_fusion.77 = (f32[2,256]{1,0:T(2,128)S(1)}, f32[2,256,1024]{2,1,0:T(8,128)S(1)}) fusion(f32[256,1024]{1,0:T(8,128)} %get-tuple-element.1394, f32[2]{0:T(128)} %get-tuple-element.1395, f32[256,1024]{1,0:T(8,128)S(1)} %get-tuple-element.1396, f32[2]{0:T(128)} %get-tuple-element.1397, f32[2,256]{1,0:T(2,128)S(1)} %fusion.372, ...), kind=kLoop, calls=%fused_computation.507.clone.1 | loop fusion | flops 72351232 | bytes 142873120 | tf_op jit(solution)/shard_map/while/body/eval_jaxpr/reduce_sum | solution.py:135
  2105.9 12.2 multiply_reduce_fusion.78
  2186.1 44.5 %multiply_multiply_fusion.4 = f32[2,261,1034]{2,1,0:T(8,128)} fusion(f32[2,256,1024]{2,1,0:T(8,128)S(1)} %copy-done.2, f32[261,1034]{1,0:T(8,128)} %fusion.373, f32[2]{0:T(128)S(1)} %get-tuple-element.1398, f32[2]{0:T(128)S(1)} %get-tuple-element.1399, f32[2]{0:T(128)S(1)} %get-tuple-element.1400, f32[2]{0:T(128)S(1)} %get-tuple-element.1401, ...), kind=kLoop, calls=%fused_computation.436.clone.1 | loop fusion | flops 71786448 | bytes 5336168 | tf_op jit(solution)/shard_map/while/body/eval_jaxpr/mul | solution.py:137
  2248.7 36.7 %multiply_reduce_fusion.77 = (f32[2,256]{1,0:T(2,128)S(1)}, f32[2,256,1024]{2,1,0:T(8,128)S(1)}) fusion(f32[256,1024]{1,0:T(8,128)} %get-tuple-element.1394, f32[2]{0:T(128)} %get-tuple-element.1395, f32[256,1024]{1,0:T(8,128)S(1)} %get-tuple-element.1396, f32[2]{0:T(128)} %get-tuple-element.1397, f32[2,256]{1,0:T(2,128)S(1)} %fusion.372, ...), kind=kLoop, calls=%fused_computation.507.clone.1 | loop fusion | flops 72351232 | bytes 142873120 | tf_op jit(solution)/shard_map/while/body/eval_jaxpr/reduce_sum | solution.py:135
  2291.1 12.2 multiply_reduce_fusion.78
  2371.2 44.5 %multiply_multiply_fusion.4 = f32[2,261,1034]{2,1,0:T(8,128)} fusion(f32[2,256,1024]{2,1,0:T(8,128)S(1)} %copy-done.2, f32[261,1034]{1,0:T(8,128)} %fusion.373, f32[2]{0:T(128)S(1)} %get-tuple-element.1398, f32[2]{0:T(128)S(1)} %get-tuple-element.1399, f32[2]{0:T(128)S(1)} %get-tuple-element.1400, f32[2]{0:T(128)S(1)} %get-tuple-element.1401, ...), kind=kLoop, calls=%fused_computation.436.clone.1 | loop fusion | flops 71786448 | bytes 5336168 | tf_op jit(solution)/shard_map/while/body/eval_jaxpr/mul | solution.py:137
  2433.9 36.7 %multiply_reduce_fusion.77 = (f32[2,256]{1,0:T(2,128)S(1)}, f32[2,256,1024]{2,1,0:T(8,128)S(1)}) fusion(f32[256,1024]{1,0:T(8,128)} %get-tuple-element.1394, f32[2]{0:T(128)} %get-tuple-element.1395, f32[256,1024]{1,0:T(8,128)S(1)} %get-tuple-element.1396, f32[2]{0:T(128)} %get-tuple-element.1397, f32[2,256]{1,0:T(2,128)S(1)} %fusion.372, ...), kind=kLoop, calls=%fused_computation.507.clone.1 | loop fusion | flops 72351232 | bytes 142873120 | tf_op jit(solution)/shard_map/while/body/eval_jaxpr/reduce_sum | solution.py:135
  2476.3 12.2 multiply_reduce_fusion.78
  2556.4 44.5 %multiply_multiply_fusion.4 = f32[2,261,1034]{2,1,0:T(8,128)} fusion(f32[2,256,1024]{2,1,0:T(8,128)S(1)} %copy-done.2, f32[261,1034]{1,0:T(8,128)} %fusion.373, f32[2]{0:T(128)S(1)} %get-tuple-element.1398, f32[2]{0:T(128)S(1)} %get-tuple-element.1399, f32[2]{0:T(128)S(1)} %get-tuple-element.1400, f32[2]{0:T(128)S(1)} %get-tuple-element.1401, ...), kind=kLoop, calls=%fused_computation.436.clone.1 | loop fusion | flops 71786448 | bytes 5336168 | tf_op jit(solution)/shard_map/while/body/eval_jaxpr/mul | solution.py:137
  2649.2 41.8 %collective-permute-done.10 = bf16[256,3072]{0,1:T(8,128)(2,1)} collective-permute-done((bf16[256,3072]{0,1:T(8,128)(2,1)}, bf16[256,3072]{0,1:T(8,128)(2,1)}, u32[]{:S(2)}, u32[]{:S(2)}) %collective-permute-start.10) | collective-permute-done | bytes 1572896 | tf_op jit(solution)/shard_map/ppermute | solution.py:30
  2690.9 32.9 %collective-permute-done.9 = bf16[256,3072]{0,1:T(8,128)(2,1)} collective-permute-done((bf16[256,3072]{0,1:T(8,128)(2,1)}, bf16[256,3072]{0,1:T(8,128)(2,1)}, u32[]{:S(2)}, u32[]{:S(2)}) %collective-permute-start.9) | collective-permute-done | bytes 1572896 | tf_op jit(solution)/shard_map/ppermute | solution.py:30
  2757.8 139.1 %reduce-scatter.9.cloned.1.call-done = bf16[192,4608]{1,0:T(8,128)(2,1)} async-done(((bf16[1536,4608]{1,0:T(8,128)(2,1)}), bf16[192,4608]{1,0:T(8,128)(2,1)}) %reduce-scatter.9.cloned.1.call-update) | async-done | bytes 1769488 | tf_op jit(solution)/shard_map/reduce_scatter | solution.py:355
  2908.7 40.1 %all-reduce.2 = (f32[16,6,11]{2,0,1:T(8,128)S(1)}, f32[8,2,2]{0,2,1:T(2,128)}, f32[1536]{0:T(1024)}, f32[1536]{0:T(1024)}, f32[1536]{0:T(1024)}) all-reduce(f32[16,6,11]{2,0,1:T(8,128)S(1)} %bitcast.778, f32[8,2,2]{0,2,1:T(2,128)S(1)} %copy.255, f32[1536]{0:T(1024)S(1)} %get-tuple-element.619, ...), channel_id=1, replica_groups=mesh['rep'=4,'seq'=8] {'rep','seq'}, use_global_device_ids=true, to_apply=%region_89.90 | all-reduce | flops 5696 | bytes 45568 | tf_op jit(solution)/shard_map/psum | solution.py:363
  2952.4 102.6 %all-reduce.6.cloned.1.call-done = (bf16[192,4608]{1,0:T(8,128)(2,1)}, bf16[192,1536]{1,0:T(8,128)(2,1)}, bf16[1536,512]{1,0:T(8,128)(2,1)}, bf16[1536,512]{1,0:T(8,128)(2,1)}, bf16[512,1536]{1,0:T(8,128)(2,1)}) async-done(((bf16[192,4608]{1,0:T(8,128)(2,1)}, bf16[192,1536]{1,0:T(8,128)(2,1)}, bf16[1536,512]{1,0:T(8,128)(2,1)}, bf16[1536,512]{1,0:T(8,128)(2,1)}, bf16[512,1536]{1,0:T(8,128)(2,1)}), ...) | async-done | bytes 7077904 | tf_op jit(solution)/shard_map/psum | solution.py:367
  (2710 shorter events, 1066.5 us)
Async XLA Ops:
  7.2 925.2 %copy-start = (bf16[1536,512]{1,0:T(8,128)(2,1)S(1)}, bf16[1536,512]{1,0:T(8,128)(2,1)}, u32[]{:S(2)}) copy-start(bf16[1536,512]{1,0:T(8,128)(2,1)} %param.28) | copy-start | bytes 4718596
  7.2 134.9 %copy-start.111 = (f32[1536]{0:T(1024)S(1)}, f32[1536]{0:T(1024)}, u32[]{:S(2)}) copy-start(f32[1536]{0:T(1024)} %param.25) | copy-start | bytes 18436
  7.2 134.8 %all-gather.4.cloned.1.call-start = ((), (), s32[]{:S(2)}) async-start(), calls=%async_computation.4 | async-start | bytes 15925248 | tf_op jit(solution)/shard_map/all_gather | solution.py:225
  8.0 646.5 %all-gather.6.cloned.1.call-start = ((), (), s32[]{:S(2)}) async-start(), calls=%async_computation.5 | async-start | bytes 5308416 | tf_op jit(solution)/shard_map/all_gather | solution.py:226
  8.7 768.8 %all-gather.8.cloned.1.call-start = ((), (), s32[]{:S(2)}) async-start(), calls=%async_computation.7 | async-start | bytes 7077888 | tf_op jit(solution)/shard_map/all_gather | solution.py:282
  9.7 141.6 %copy-start.119 = (f32[256]{0:T(256)}, f32[256]{0:T(256)S(1)}, u32[]{:S(2)}) copy-start(f32[256]{0:T(256)S(1)} %get-tuple-element.871) | copy-start | bytes 3076
  152.7 12.5 copy-start.130
  154.1 14.3 copy-start.116
  154.1 15.5 copy-start.132
  154.1 67.7 %collective-permute-start = (bf16[256,3072]{1,0:T(8,128)(2,1)}, bf16[256,3072]{1,0:T(8,128)(2,1)}, u32[]{:S(2)}, u32[]{:S(2)}) collective-permute-start(bf16[256,3072]{1,0:T(8,128)(2,1)} %slice.2477), channel_id=1, source_target_pairs={{0,3},{1,4},{2,5},{3,6},{4,7},{8,11},{9,12},{10,13},{11,14},{12,15... | collective-permute-start | bytes 4718600 | tf_op jit(solution)/shard_map/ppermute | solution.py:30
  156.7 119.3 %collective-permute-start.1 = (bf16[256,3072]{1,0:T(8,128)(2,1)}, bf16[256,3072]{1,0:T(8,128)(2,1)}, u32[]{:S(2)}, u32[]{:S(2)}) collective-permute-start(bf16[256,3072]{1,0:T(8,128)(2,1)} %slice.2477), channel_id=1, source_target_pairs={{0,2},{1,3},{2,4},{3,5},{4,6},{5,7},{8,10},{9,11},{10,12},{11,13},... | collective-permute-start | bytes 4718600 | tf_op jit(solution)/shard_map/ppermute | solution.py:30
  161.4 114.6 %collective-permute-start.2 = (bf16[256,3072]{1,0:T(8,128)(2,1)}, bf16[256,3072]{1,0:T(8,128)(2,1)}, u32[]{:S(2)}, u32[]{:S(2)}) collective-permute-start(bf16[256,3072]{1,0:T(8,128)(2,1)} %slice.2477), channel_id=1, source_target_pairs={{0,1},{1,2},{2,3},{3,4},{4,5},{5,6},{6,7},{8,9},{9,10},{10,11},{11... | collective-permute-start | bytes 4718600 | tf_op jit(solution)/shard_map/ppermute | solution.py:30
  165.1 862.6 %reduce-scatter.7.cloned.1.call-start = ((), (), s32[]{:S(2)}) async-start(), calls=%async_computation.8 | async-start | bytes 7077888 | tf_op jit(solution)/shard_map/reduce_scatter | solution.py:296
  166.7 4.2 collective-permute-start.3
  658.8 55.2 %copy-start.16 = (f32[256,1536]{1,0:T(8,128)}, f32[256,1536]{1,0:T(8,128)S(1)}, u32[]{:S(2)}) copy-start(f32[256,1536]{1,0:T(8,128)S(1)} %get-tuple-element.875) | copy-start | bytes 4718596
  660.1 53.8 %collective-permute-start.4 = (bf16[256,1536]{1,0:T(8,128)(2,1)S(1)}, bf16[256,1536]{1,0:T(8,128)(2,1)S(1)}, u32[]{:S(2)}, u32[]{:S(2)}) collective-permute-start(bf16[256,1536]{1,0:T(8,128)(2,1)S(1)} %get-tuple-element.713), channel_id=1, source_target_pairs={{0,7},{1,0},{2,1},{3,2},{4,3},{5,4},{6,5},{7,6},{8,15},{9,8},{10,9... | collective-permute-start | bytes 2359304 | tf_op jit(solution)/shard_map/ppermute | solution.py:17
  713.9 46.6 %copy-start.18 = (bf16[256,1536]{1,0:T(8,128)(2,1)}, bf16[256,1536]{1,0:T(8,128)(2,1)S(1)}, u32[]{:S(2)}) copy-start(bf16[256,1536]{1,0:T(8,128)(2,1)S(1)} %collective-permute-done.4) | copy-start | bytes 2359300
  714.0 44.5 %collective-permute-start.5 = (bf16[512,1536]{1,0:T(8,128)(2,1)S(1)}, bf16[512,1536]{1,0:T(8,128)(2,1)S(1)}, u32[]{:S(2)}, u32[]{:S(2)}) collective-permute-start(bf16[512,1536]{1,0:T(8,128)(2,1)S(1)} %pad_maximum_fusion.5), channel_id=1, source_target_pairs={{0,6},{1,7},{2,0},{3,1},{4,2},{5,3},{6,4},{7,5},{8,14},{9,15},{10,... | collective-permute-start | bytes 4718600 | tf_op jit(solution)/shard_map/ppermute | solution.py:17
  760.7 152.8 %collective-permute-start.6 = (bf16[1024,1536]{1,0:T(8,128)(2,1)}, bf16[1024,1536]{1,0:T(8,128)(2,1)}, u32[]{:S(2)}, u32[]{:S(2)}) collective-permute-start(bf16[1024,1536]{1,0:T(8,128)(2,1)} %pad_maximum_fusion.3), channel_id=1, source_target_pairs={{0,4},{1,5},{2,6},{3,7},{4,0},{5,1},{6,2},{7,3},{8,12},{9,13},{10,... | collective-permute-start | bytes 9437192 | tf_op jit(solution)/shard_map/ppermute | solution.py:17
  956.2 141.9 %reduce-scatter.5.cloned.1.call-start = ((), (), s32[]{:S(2)}) async-start(), calls=%async_computation.6 | async-start | bytes 7077888 | tf_op jit(solution)/shard_map/reduce_scatter | solution.py:275
  964.4 63.3 %copy-start.17 = (f32[256,1536]{1,0:T(8,128)S(1)}, f32[256,1536]{1,0:T(8,128)}, u32[]{:S(2)}) copy-start(f32[256,1536]{1,0:T(8,128)} %copy-done.16) | copy-start | bytes 4718596
  964.5 133.6 %copy-start.25 = (bf16[1,256,1536]{2,1,0:T(8,128)(2,1)S(1)}, bf16[1,256,1536]{2,1,0:T(8,128)(2,1)}, u32[]{:S(2)}) copy-start(bf16[1,256,1536]{2,1,0:T(8,128)(2,1)} %param.31) | copy-start | bytes 2359300
  964.5 1793.3 %reduce-scatter.11.cloned.1.call-start = ((), (), s32[]{:S(2)}) async-start(), calls=%async_computation.10 | async-start | bytes 5308416 | tf_op jit(solution)/shard_map/reduce_scatter | solution.py:358
  1126.4 1770.5 %reduce-scatter.9.cloned.1.call-start = ((), (), s32[]{:S(2)}) async-start(), calls=%async_computation.9 | async-start | bytes 15925248 | tf_op jit(solution)/shard_map/reduce_scatter | solution.py:355
  1200.5 11.5 copy-start.121
  1233.5 21.4 copy-start.6
  1385.7 11.5 copy-start.121
  1418.7 21.4 copy-start.6
  1570.9 11.5 copy-start.121
  1603.9 21.4 copy-start.6
  1789.1 21.4 copy-start.6
  1974.2 21.4 copy-start.6
  2159.4 21.4 copy-start.6
  2344.6 21.4 copy-start.6
  2496.8 11.5 copy-start.121
  2529.8 21.4 copy-start.6
  2635.9 55.1 %collective-permute-start.10 = (bf16[256,3072]{0,1:T(8,128)(2,1)}, bf16[256,3072]{0,1:T(8,128)(2,1)}, u32[]{:S(2)}, u32[]{:S(2)}) collective-permute-start(bf16[256,3072]{0,1:T(8,128)(2,1)} %get-tuple-element.860), channel_id=1, source_target_pairs={{3,0},{4,1},{5,2},{6,3},{7,4},{11,8},{12,9},{13,10},{14,11},{15,12... | collective-permute-start | bytes 4718600 | tf_op jit(solution)/shard_map/ppermute | solution.py:30
  2637.1 53.8 %collective-permute-start.8 = (bf16[256,3072]{0,1:T(8,128)(2,1)}, bf16[256,3072]{0,1:T(8,128)(2,1)}, u32[]{:S(2)}, u32[]{:S(2)}) collective-permute-start(bf16[256,3072]{0,1:T(8,128)(2,1)} %get-tuple-element.859), channel_id=1, source_target_pairs={{1,0},{2,1},{3,2},{4,3},{5,4},{6,5},{7,6},{9,8},{10,9},{11,10},{12... | collective-permute-start | bytes 4718600 | tf_op jit(solution)/shard_map/ppermute | solution.py:30
  2638.4 85.4 %collective-permute-start.9 = (bf16[256,3072]{0,1:T(8,128)(2,1)}, bf16[256,3072]{0,1:T(8,128)(2,1)}, u32[]{:S(2)}, u32[]{:S(2)}) collective-permute-start(bf16[256,3072]{0,1:T(8,128)(2,1)} %get-tuple-element.861), channel_id=1, source_target_pairs={{2,0},{3,1},{4,2},{5,3},{6,4},{7,5},{10,8},{11,9},{12,10},{13,11},... | collective-permute-start | bytes 4718600 | tf_op jit(solution)/shard_map/ppermute | solution.py:30
  2644.4 3.8 collective-permute-start.7
  2649.1 78.7 %copy-start.22 = (bf16[1,256,1536]{2,1,0:T(8,128)(2,1)S(1)}, bf16[1,256,1536]{2,1,0:T(8,128)(2,1)}, u32[]{:S(2)}) copy-start(bf16[1,256,1536]{2,1,0:T(8,128)(2,1)} %param.18) | copy-start | bytes 2359300
  2649.1 78.7 %copy-start.26 = (bf16[251,8,2,96]{0,3,2,1:T(8,128)(2,1)S(1)}, bf16[251,8,2,96]{0,3,2,1:T(8,128)(2,1)}, u32[]{:S(2)}) copy-start(bf16[251,8,2,96]{0,3,2,1:T(8,128)(2,1)} %slice.3701) | copy-start | bytes 2313220
  2649.2 78.7 %copy-start.112 = (f32[1536]{0:T(1024)S(1)}, f32[1536]{0:T(1024)}, u32[]{:S(2)}) copy-start(f32[1536]{0:T(1024)} %param.25) | copy-start | bytes 18436
  2649.2 78.8 %copy-start.120 = (f32[256]{0:T(256)S(1)}, f32[256]{0:T(256)}, u32[]{:S(2)}) copy-start(f32[256]{0:T(256)} %copy-done.119) | copy-start | bytes 3076
  2737.1 317.9 %all-reduce.6.cloned.1.call-start = ((), (), s32[]{:S(2)}) async-start(), calls=%async_computation.11 | async-start | bytes 14155776 | tf_op jit(solution)/shard_map/psum | solution.py:367
  2737.1 15.9 slice-start
  2897.7 51.9 %copy-start.11 = (f32[256,1536]{1,0:T(8,128)S(1)}, f32[256,1536]{1,0:T(8,128)}, u32[]{:S(2)}) copy-start(f32[256,1536]{1,0:T(8,128)} %copy-done.10) | copy-start | bytes 4718596
  2897.7 51.9 %copy-start.131 = (f32[256]{0:T(256)S(1)}, f32[256]{0:T(256)}, u32[]{:S(2)}) copy-start(f32[256]{0:T(256)} %get-tuple-element.870) | copy-start | bytes 3076
  (756 other events, 5293.5 us)
Sparse Core Ops, SparseCore 0:
  9.7 132.3 all-gather.3
  143.7 75.9 all-gather.5
  221.9 99.1 all-gather.7
  956.3 71.3 reduce-scatter.6
  1029.8 68.1 reduce-scatter.4
  1126.5 53.3 reduce-scatter.10
  2737.2 159.6 reduce-scatter.8
  2902.3 152.6 all-reduce.5
